TPU v7x, 128 devices: a whole 4x4x4 slice. The times are simulated.
128 devices in a mesh: dp: 8 (over z, core), expert: 16 (over y, x).
Axes of the slice: x: 4, y: 4, z: 4, core: 2. Of those that a mesh axis runs over, the one named last changes fastest.
Arguments:
- inputs: bfloat16 [16384, 2048], P(('dp', 'expert')), may hold values from -6 to 6
- out_grad: bfloat16 [16384, 2048], P(('dp', 'expert')), may hold values from -6 to 6
- combine: float32 [16384, 8], P(('dp', 'expert')), may hold values from 0 to 1, as said below
- routes: int32 [16384, 8], P(('dp', 'expert')), may hold values from 0 to 63, all different within a row; in each aligned block of 128 rows (0 to 127, 128 to 255, ...) at most 24 rows name the same one
- saved_hidden: bfloat16 [8, 64, 16, 24, 768], P('dp', 'expert'), may hold values from -6 to 6
- down_weight: bfloat16 [64, 2048, 768], P('expert'), may hold values from -0.21875 to 0.21875
- router_weight: bfloat16 [64, 2048], replicated, may hold values from -0.125 to 0.125
Outputs:
- hidden_grad: bfloat16 [8, 64, 16, 24, 768], P('dp', 'expert')
- down_grad: bfloat16 [64, 2048, 768], P('expert', 'dp')
- input_grad: bfloat16 [16384, 2048], P(('dp', 'expert'))
- router_grad: float32 [64, 2048], replicated
Inputs may be any that keep to these rules, and one draw needn't show every extreme that they name: `routes`: each token names 8 different experts; among the 128 tokens of one device no expert is named by more than 24 tokens, a bound that some block reaches. `combine`: each token's 8 weights are positive and sum to one.
All inputs are finite; a program needn't handle non-finite values.
Results may differ from a plain program's by a relative error of at most 0.017.
Values may be sent and summed in bfloat16 or wider, within the bound.
A program may use at most 128 MiB of HBM per device.

v0:
```python
import jax
import jax.numpy as jnp
from jax import lax
from jax.sharding import PartitionSpec as P


def make_marks(block_routes, total_experts):
    return block_routes[:, :, None] == jnp.arange(total_experts, dtype=jnp.int32)[None, None, :]


def slot_positions(route_marks):
    counts = jnp.sum(route_marks.astype(jnp.bfloat16), axis=1)
    token_order = jnp.arange(route_marks.shape[0], dtype=jnp.int32)
    earlier = (token_order[None, :] < token_order[:, None]).astype(jnp.bfloat16)
    before = jnp.dot(earlier, counts, preferred_element_type=jnp.float32)
    picked = jnp.sum(jnp.where(route_marks, before[:, None, :], 0.0), axis=2)
    return picked.astype(jnp.int32)


def pack_rows(scaled, lane_index, owner_slot, positions, local_experts, groups, capacity):
    width = scaled.shape[-1]
    flat_index = (owner_slot * groups + lane_index) * capacity + positions
    zero_rows = jnp.zeros((local_experts * groups * capacity, width), jnp.bfloat16)
    filled = zero_rows.at[flat_index.reshape(-1)].set(scaled.reshape(-1, width))
    return filled.reshape(local_experts, groups, capacity, width)


def local(inputs, out_grad, combine, routes, saved_hidden, down_weight, router_weight):
    token_count, width = out_grad.shape
    local_experts = down_weight.shape[0]
    total_experts = router_weight.shape[0]
    groups = lax.axis_size("expert")
    capacity = saved_hidden.shape[3]
    hidden_width = saved_hidden.shape[4]
    route_marks = make_marks(routes, total_experts)
    positions = slot_positions(route_marks)
    owner_dev = routes // local_experts
    owner_slot = routes % local_experts
    scaled = (combine[:, :, None] * out_grad[:, None, :].astype(jnp.float32)).astype(jnp.bfloat16)
    packed = pack_rows(scaled, owner_dev, owner_slot, positions, local_experts, groups, capacity)
    received = lax.all_to_all(packed, "expert", split_axis=1, concat_axis=1, tiled=True)
    hidden_local = saved_hidden[0]
    products_list = []
    hidden_list = []
    weight_terms = []
    for expert in range(local_experts):
        slot_rows = received[expert].reshape(groups * capacity, width)
        slot_acts = hidden_local[expert].reshape(groups * capacity, hidden_width)
        weight = down_weight[expert]
        recomputed = lax.dot_general(
            slot_acts, weight, (((1,), (1,)), ((), ())), preferred_element_type=jnp.float32
        )
        products_list.append(jnp.sum(recomputed * slot_rows.astype(jnp.float32), axis=1))
        hidden_list.append(
            jnp.dot(slot_rows, weight, preferred_element_type=jnp.float32).astype(jnp.bfloat16)
        )
        weight_terms.append(
            lax.dot_general(
                slot_rows, slot_acts, (((0,), (0,)), ((), ())), preferred_element_type=jnp.float32
            )
        )
    down_grad = lax.psum_scatter(
        jnp.stack(weight_terms).astype(jnp.bfloat16), "dp", scatter_dimension=1, tiled=True
    )
    hidden_grad = jnp.stack(hidden_list).reshape(1, local_experts, groups, capacity, hidden_width)
    slot_products = jnp.stack(products_list).reshape(local_experts, groups, capacity)
    returned = lax.all_to_all(slot_products, "expert", split_axis=1, concat_axis=1, tiled=True)
    pair_index = (owner_slot * groups + owner_dev) * capacity + positions
    pair_sums = returned.reshape(-1)[pair_index]
    logit_grad = pair_sums - combine * jnp.sum(pair_sums, axis=1, keepdims=True)
    dense_grad = jnp.sum(jnp.where(route_marks, logit_grad[:, :, None], 0.0), axis=1).astype(
        jnp.bfloat16
    )
    input_grad = jnp.dot(dense_grad, router_weight, preferred_element_type=jnp.float32).astype(
        jnp.bfloat16
    )
    router_part = lax.dot_general(
        dense_grad, inputs, (((0,), (0,)), ((), ())), preferred_element_type=jnp.float32
    )
    router_grad = lax.psum(router_part, ("dp", "expert"))
    return (hidden_grad, down_grad, input_grad, router_grad)


def solution(mesh):
    placed = (
        P(("dp", "expert"), None),
        P(("dp", "expert"), None),
        P(("dp", "expert"), None),
        P(("dp", "expert"), None),
        P("dp", "expert", None, None, None),
        P("expert", None, None),
        P(),
    )
    return jax.shard_map(
        local,
        mesh=mesh,
        in_specs=placed,
        out_specs=(
            P("dp", "expert", None, None, None),
            P("expert", "dp", None),
            P(("dp", "expert"), None),
            P(),
        ),
        check_vma=False,
    )
```

profile of v0, /device:TPU:1, one launch (start us, length us, event | category | flops | bytes accessed | tf_op | source)
XLA Modules:
  0.0 366.2 jit_solution(16921963926218966697)
XLA Ops:
  8.0 0.8 fusion.55
  8.9 0.7 select_reduce_fusion.1
  9.7 0.7 compare_select_fusion.1
  10.6 0.8 copy.46
  11.5 1.1 convert_element_type.50
  12.6 10.6 %scatter_custom_fusion = bf16[1536,2048]{1,0:T(8,128)(2,1)} fusion(s32[1024]{0:T(1024)S(1)} %bitcast.110, f32[128,2048]{1,0:T(8,128)S(1)} %convert_element_type.50, f32[1024]{0:T(1024)S(1)} %mul.48, bf16[]{:T(256)} %constant.31.clone.1), kind=kCustom, calls=%fused_computation.5 | custom fusion | flops 4194304 | bytes 7344130 | tf_op jit(solution)/shard_map/scatter | solution.py:24
  23.2 6.6 %copy.47 = bf16[4,16,24,2048]{3,2,0,1:T(8,128)(2,1)} copy(bf16[4,16,24,2048]{3,2,1,0:T(8,128)(2,1)} %bitcast.85) | data formatting | bytes 12582912 | tf_op jit(solution)/shard_map/reshape | solution.py:25
  29.8 7.8 %all-to-all-start = ((bf16[4,16,24,2048]{3,2,0,1:T(8,128)(2,1)}), bf16[4,16,24,2048]{3,2,0,1:T(8,128)(2,1)}, u32[]{:S(2)}, u32[]{:S(2)}) async-start(bf16[4,16,24,2048]{3,2,0,1:T(8,128)(2,1)} %copy.47), calls=%async_computation | async-start | bytes 12582912 | tf_op jit(solution)/shard_map/all_to_all | solution.py:41
  37.8 1.2 fusion.70
  39.0 90.8 %all-to-all-done = bf16[4,16,24,2048]{3,2,0,1:T(8,128)(2,1)} async-done(((bf16[4,16,24,2048]{3,2,0,1:T(8,128)(2,1)}), bf16[4,16,24,2048]{3,2,0,1:T(8,128)(2,1)}, u32[]{:S(2)}, u32[]{:S(2)}) %all-to-all-start) | async-done | bytes 6291488 | tf_op jit(solution)/shard_map/all_to_all | solution.py:41
  129.9 4.8 %fusion.69 = (bf16[1,16,24,2048]{3,2,0,1:T(8,128)(2,1)S(1)}, bf16[1,16,24,2048]{3,2,0,1:T(8,128)(2,1)}, bf16[1,16,24,2048]{3,2,0,1:T(8,128)(2,1)S(1)}, bf16[1,16,24,2048]{3,2,0,1:T(8,128)(2,1)S(1)}) fusion(bf16[4,16,24,2048]{3,2,0,1:T(8,128)(2,1)} %all-to-all-done), kind=kLoop, calls=%fused_computation.80 | loop fusion | bytes 12582912 | tf_op jit(solution)/shard_map/slice | solution.py:47
  134.7 3.5 fusion.23
  138.2 3.6 multiply_reduce_fusion.2
  141.9 1.5 multiply_reduce_fusion.1
  143.4 3.5 fusion.24
  146.9 1.5 multiply_reduce_fusion.3
  148.4 3.5 fusion.22
  152.2 3.9 %multiply_reduce_fusion = f32[384]{0:T(512)S(1)} fusion(bf16[384,2048]{1,0:T(8,128)(2,1)} %bitcast.95, bf16[384,768]{1,0:T(8,128)(2,1)S(1)} %bitcast.98, bf16[4,2048,768]{2,1,0:T(8,128)(2,1)} %param.12), kind=kOutput, calls=%fused_computation.28 | convolution fusion | flops 1210318464 | bytes 5309952 | tf_op jit(solution)/shard_map/dot_general | solution.py:50
  156.9 5.4 %all-to-all-start.1 = ((f32[4,16,24]{2,0,1:T(4,128)}), f32[4,16,24]{2,0,1:T(4,128)S(1)}, u32[]{:S(2)}, u32[]{:S(2)}) async-start(f32[4,16,24]{2,0,1:T(4,128)} %pad_maximum_fusion.2), calls=%async_computation.2 | async-start | bytes 65536 | tf_op jit(solution)/shard_map/all_to_all | solution.py:67
  162.6 4.9 %fusion.25 = bf16[1,2048,768]{2,1,0:T(8,128)(2,1)} fusion(bf16[384,2048]{1,0:T(8,128)(2,1)} %bitcast.96, bf16[384,768]{1,0:T(8,128)(2,1)S(1)} %bitcast.99), kind=kOutput, calls=%fused_computation.36 | convolution fusion | flops 1209532416 | bytes 5308416 | tf_op jit(solution)/shard_map/dot_general | solution.py:58
  167.5 1.3 all-to-all-done.1
  168.8 6.2 %gather_fusion = f32[1024]{0:T(1024)S(1)} fusion(f32[1536]{0:T(1024)S(1)} %reshape.84, s32[1024]{0:T(1024)S(1)} %broadcast_clamp_fusion), kind=kCustom, calls=%fused_computation | custom fusion | bytes 12288 | tf_op jit(solution)/shard_map/gather | solution.py:69
  175.4 1.0 fusion.71
  176.5 10.7 %pad_maximum_fusion = bf16[4,2048,768]{2,1,0:T(8,128)(2,1)} fusion(bf16[1,2048,768]{2,1,0:T(8,128)(2,1)} %fusion.25, bf16[1,2048,768]{2,1,0:T(8,128)(2,1)} %fusion.24, bf16[1,2048,768]{2,1,0:T(8,128)(2,1)} %fusion.23, bf16[1,2048,768]{2,1,0:T(8,128)(2,1)} %fusion.22), kind=kLoop, calls=%fused_computation.2 | loop fusion | flops 18874368 | bytes 25165824 | tf_op jit(solution)/shard_map/stack | solution.py:63
  187.2 3.9 %fusion.51 = bf16[384,768]{1,0:T(8,128)(2,1)S(1)} fusion(bf16[384,2048]{1,0:T(8,128)(2,1)} %bitcast.97, bf16[4,2048,768]{2,1,0:T(8,128)(2,1)} %param.12), kind=kOutput, calls=%fused_computation.50 | convolution fusion | flops 1208254464 | bytes 5308416 | tf_op jit(solution)/shard_map/dot_general | solution.py:55
  191.1 3.4 fusion.42
  194.6 3.3 fusion.48
  197.9 4.1 %fusion.45 = bf16[384,768]{1,0:T(8,128)(2,1)S(1)} fusion(bf16[384,2048]{1,0:T(8,128)(2,1)S(1)} %bitcast.88, bf16[4,2048,768]{2,1,0:T(8,128)(2,1)} %param.12), kind=kOutput, calls=%fused_computation.48 | convolution fusion | flops 1208254464 | bytes 5308416 | tf_op jit(solution)/shard_map/dot_general | solution.py:55
  202.0 1.7 pad_maximum_fusion.1
  203.7 1.1 convolution_convert_fusion.4
  204.9 152.0 %all-reduce.2.cloned.1.call-done = f32[64,2048]{1,0:T(8,128)} async-done(((f32[64,2048]{1,0:T(8,128)}), f32[64,2048]{1,0:T(8,128)}) %all-reduce.2.cloned.1.call-update) | async-done | bytes 524304 | tf_op jit(solution)/shard_map/psum | solution.py:80
  356.9 1.9 copy.52
  (56 shorter events, 2.5 us)
Async XLA Ops:
  8.0 167.4 %copy-start = (bf16[128,2048]{1,0:T(8,128)(2,1)S(1)}, bf16[128,2048]{1,0:T(8,128)(2,1)}, u32[]{:S(2)}) copy-start(bf16[128,2048]{1,0:T(8,128)(2,1)} %param.7) | copy-start | bytes 1572868
  29.8 8.0 %copy-start.1 = (bf16[1,4,16,24,768]{4,3,2,1,0:T(8,128)(2,1)S(1)}, bf16[1,4,16,24,768]{4,3,2,1,0:T(8,128)(2,1)}, u32[]{:S(2)}) copy-start(bf16[1,4,16,24,768]{4,3,2,1,0:T(8,128)(2,1)} %param.11) | copy-start | bytes 7077892
  29.8 100.1 %all-to-all-start = ((bf16[4,16,24,2048]{3,2,0,1:T(8,128)(2,1)}), bf16[4,16,24,2048]{3,2,0,1:T(8,128)(2,1)}, u32[]{:S(2)}, u32[]{:S(2)}) async-start(bf16[4,16,24,2048]{3,2,0,1:T(8,128)(2,1)} %copy.47), calls=%async_computation | async-start | bytes 12582912 | tf_op jit(solution)/shard_map/all_to_all | solution.py:41
  39.0 95.7 %copy-start.8 = (bf16[1,1,16,24,768]{4,3,2,1,0:T(8,128)(2,1)S(1)}, bf16[1,1,16,24,768]{4,3,2,1,0:T(8,128)(2,1)}, u32[]{:S(2)}) copy-start(bf16[1,1,16,24,768]{4,3,2,1,0:T(8,128)(2,1)} %get-tuple-element.11) | copy-start | bytes 1769476
  129.9 11.9 %slice-start = ((s8[12582912]{0:T(1024)(128)(4,1)}), s8[4194304]{0:T(1024)(128)(4,1)S(1)}, s32[]{:S(2)}) async-start(s8[12582912]{0:T(1024)(128)(4,1)} %bitcast.111), calls=%async_computation.5 | async-start | bytes 8388608
  129.9 11.9 %slice-start.1 = ((s8[12582912]{0:T(1024)(128)(4,1)}), s8[4194304]{0:T(1024)(128)(4,1)S(1)}, s32[]{:S(2)}) async-start(s8[12582912]{0:T(1024)(128)(4,1)} %bitcast.111), calls=%async_computation.6 | async-start | bytes 8388608
  134.7 8.7 %copy-start.2 = (bf16[1,16,24,2048]{3,2,0,1:T(8,128)(2,1)}, bf16[1,16,24,2048]{3,2,0,1:T(8,128)(2,1)S(1)}, u32[]{:S(2)}) copy-start(bf16[1,16,24,2048]{3,2,0,1:T(8,128)(2,1)S(1)} %get-tuple-element.8) | copy-start | bytes 4718596
  134.7 13.7 %copy-start.4 = (bf16[1,16,24,2048]{3,2,0,1:T(8,128)(2,1)}, bf16[1,16,24,2048]{3,2,0,1:T(8,128)(2,1)S(1)}, u32[]{:S(2)}) copy-start(bf16[1,16,24,2048]{3,2,0,1:T(8,128)(2,1)S(1)} %get-tuple-element.6) | copy-start | bytes 4718596
  138.2 3.6 copy-start.7
  138.2 3.6 slice-start.2
  143.4 3.5 copy-start.6
  156.9 11.8 %all-to-all-start.1 = ((f32[4,16,24]{2,0,1:T(4,128)}), f32[4,16,24]{2,0,1:T(4,128)S(1)}, u32[]{:S(2)}, u32[]{:S(2)}) async-start(f32[4,16,24]{2,0,1:T(4,128)} %pad_maximum_fusion.2), calls=%async_computation.2 | async-start | bytes 65536 | tf_op jit(solution)/shard_map/all_to_all | solution.py:67
  162.3 194.6 %all-reduce.2.cloned.1.call-start = ((), (), s32[]{:S(2)}) async-start(), calls=%async_computation.4 | async-start | bytes 1048576 | tf_op jit(solution)/shard_map/psum | solution.py:80
  168.8 6.5 %copy-start.11 = (f32[128,8]{0,1:T(8,128)S(1)}, f32[128,8]{0,1:T(8,128)}, u32[]{:S(2)}) copy-start(f32[128,8]{0,1:T(8,128)} %param.9) | copy-start | bytes 12292
  168.8 6.5 %copy-start.10 = (s32[128,8]{0,1:T(8,128)S(1)}, s32[128,8]{0,1:T(8,128)}, u32[]{:S(2)}) copy-start(s32[128,8]{0,1:T(8,128)} %param.10) | copy-start | bytes 12292
  176.4 180.5 %reduce-scatter.2.cloned.1.call-start = ((), (), s32[]{:S(2)}) async-start(), calls=%async_computation.3 | async-start | bytes 14155776 | tf_op jit(solution)/shard_map/reduce_scatter | solution.py:62
  187.2 3.9 %copy-start.5 = (bf16[1,16,24,2048]{3,2,0,1:T(8,128)(2,1)S(1)}, bf16[1,16,24,2048]{3,2,0,1:T(8,128)(2,1)}, u32[]{:S(2)}) copy-start(bf16[1,16,24,2048]{3,2,0,1:T(8,128)(2,1)} %copy-done.4) | copy-start | bytes 4718596
  191.1 3.5 copy-start.3
  202.0 1.7 copy-start.9
Sparse Core Ops, SparseCore 0:
  176.5 180.2 all-reduce.1
Sparse Core Ops, SparseCore 1:
  187.3 75.3 reduce-scatter.1
where the time goes:
time: 367 us; the launch traced here: 366 us
  waiting for transfers between devices  244 us (66%)
  matrix products  43 us (12%)
  other arithmetic  27.2 us (7%)
  local copies, waits for them, and re-layouts  22.6 us (6%)
  between operations  15.8 us (4%)
  starting transfers between devices  13.5 us (4%)
    psum x1, waiting for transfers between devices, local(): router_grad = lax.psum(router_part, ('dp', 'expert'))  152 us
    all_to_all x1, waiting for transfers between devices, local(): lax.all_to_all(packed, 'expert', split_axis=1, concat_axis=1, tiled=True)  90.8 us
    dot_general x4, matrix products, local(): lax.dot_general(slot_rows, slot_acts, (((0,), (0,)), ((), ())), preferred...  15.5 us
    dot_general x4, matrix products, local(): jnp.dot(slot_rows, weight, preferred_element_type=jnp.float32)  14.8 us
    another operation x1, other arithmetic, local(): jnp.stack(weight_terms).astype(jnp.bfloat16)  10.7 us
    scatter x1, other arithmetic, pack_rows(): filled = zero_rows.at[flat_index.reshape(-1)].set(scaled.reshape(-1, width))  10.6 us
    dot_general x4, matrix products, local(): lax.dot_general(slot_acts, weight, (((1,), (1,)), ((), ())), preferred_el...  10.5 us
    all_to_all x1, starting transfers between devices, local(): lax.all_to_all(packed, 'expert', split_axis=1, concat_axis=1, tiled=True)  7.77 us
  transfers between devices with their start and end apart: 4, of which 3 were waited for; matrix products, arithmetic and copies ran while one was open for 9% of the time, Pallas kernels for 0%

commit v1 on v0

--- a/solution.py
+++ b/solution.py
@@ -77,7 +77,7 @@
     router_part = lax.dot_general(
         dense_grad, inputs, (((0,), (0,)), ((), ())), preferred_element_type=jnp.float32
     )
-    router_grad = lax.psum(router_part, ("dp", "expert"))
+    router_grad = lax.psum(lax.psum(router_part, "expert"), "dp")
     return (hidden_grad, down_grad, input_grad, router_grad)
 
 

time: 367 us -> 407 us (1.11)
  waiting for transfers between devices: 244 us -> 280 us
  matrix products: 43 us -> 48.6 us
    reduce_scatter x1, waiting for transfers between devices: 0.01 us -> 76 us  [local(): lax.psum_scatter(jnp.stack(weight_terms).astype(jnp.bfloat16), 'dp', scat...]
    psum x1 -> x2, waiting for transfers between devices: 152 us -> 112 us  [local(): router_grad = lax.psum(lax.psum(router_part, 'expert'), 'dp')]
    dot_general x4, matrix products: 10.5 us -> 15.3 us  [local(): lax.dot_general(slot_acts, weight, (((1,), (1,)), ((), ())), preferred_el...]
  transfers between devices with their start and end apart: 4 -> 5, of which waited for: 3 -> 5; matrix products, arithmetic and copies ran while one was open for 9% -> 10% of each run, Pallas kernels for 0% -> 0%
where the time goes in v1:
time: 407 us
  waiting for transfers between devices  280 us (69%)
  matrix products  48.6 us (12%)
  other arithmetic  27.2 us (7%)
  local copies, waits for them, and re-layouts  23.1 us (6%)
  between operations  14 us (3%)
  starting transfers between devices  13.5 us (3%)
    psum x2, waiting for transfers between devices, local(): router_grad = lax.psum(lax.psum(router_part, 'expert'), 'dp')  112 us
    all_to_all x1, waiting for transfers between devices, local(): lax.all_to_all(packed, 'expert', split_axis=1, concat_axis=1, tiled=True)  90.8 us
    reduce_scatter x1, waiting for transfers between devices, local(): lax.psum_scatter(jnp.stack(weight_terms).astype(jnp.bfloat16), 'dp', scat...  76 us
    dot_general x4, matrix products, local(): lax.dot_general(slot_rows, slot_acts, (((0,), (0,)), ((), ())), preferred...  17.1 us
    dot_general x4, matrix products, local(): lax.dot_general(slot_acts, weight, (((1,), (1,)), ((), ())), preferred_el...  15.3 us
    dot_general x4, matrix products, local(): jnp.dot(slot_rows, weight, preferred_element_type=jnp.float32)  13.9 us
    another operation x1, other arithmetic, local(): jnp.stack(weight_terms).astype(jnp.bfloat16)  10.7 us
    scatter x1, other arithmetic, pack_rows(): filled = zero_rows.at[flat_index.reshape(-1)].set(scaled.reshape(-1, width))  10.6 us
  transfers between devices with their start and end apart: 5, of which 5 were waited for; matrix products, arithmetic and copies ran while one was open for 10% of the time, Pallas kernels for 0%

profile of v1, /device:TPU:1, one launch (start us, length us, event | category | flops | bytes accessed | tf_op | source)
XLA Modules:
  0.0 406.7 jit_solution(740968120174877481)
XLA Ops:
  7.2 0.8 fusion.55
  9.8 0.8 copy.46
  10.6 1.1 convert_element_type.50
  11.8 10.6 %scatter_custom_fusion = bf16[1536,2048]{1,0:T(8,128)(2,1)} fusion(s32[1024]{0:T(1024)S(1)} %bitcast.110, f32[128,2048]{1,0:T(8,128)S(1)} %convert_element_type.50, f32[1024]{0:T(1024)S(1)} %mul.48, bf16[]{:T(256)} %constant.31.clone.1), kind=kCustom, calls=%fused_computation.5 | custom fusion | flops 4194304 | bytes 7344130 | tf_op jit(solution)/shard_map/scatter | solution.py:24
  22.4 6.6 %copy.47 = bf16[4,16,24,2048]{3,2,0,1:T(8,128)(2,1)} copy(bf16[4,16,24,2048]{3,2,1,0:T(8,128)(2,1)} %bitcast.85) | data formatting | bytes 12582912 | tf_op jit(solution)/shard_map/reshape | solution.py:25
  29.0 7.8 %all-to-all-start = ((bf16[4,16,24,2048]{3,2,0,1:T(8,128)(2,1)}), bf16[4,16,24,2048]{3,2,0,1:T(8,128)(2,1)}, u32[]{:S(2)}, u32[]{:S(2)}) async-start(bf16[4,16,24,2048]{3,2,0,1:T(8,128)(2,1)} %copy.47), calls=%async_computation | async-start | bytes 12582912 | tf_op jit(solution)/shard_map/all_to_all | solution.py:41
  37.0 1.2 fusion.70
  38.2 90.8 %all-to-all-done = bf16[4,16,24,2048]{3,2,0,1:T(8,128)(2,1)} async-done(((bf16[4,16,24,2048]{3,2,0,1:T(8,128)(2,1)}), bf16[4,16,24,2048]{3,2,0,1:T(8,128)(2,1)}, u32[]{:S(2)}, u32[]{:S(2)}) %all-to-all-start) | async-done | bytes 6291488 | tf_op jit(solution)/shard_map/all_to_all | solution.py:41
  129.0 5.3 %fusion.69 = (bf16[1,16,24,2048]{3,2,0,1:T(8,128)(2,1)}, bf16[1,16,24,2048]{3,2,0,1:T(8,128)(2,1)}, bf16[1,16,24,2048]{3,2,0,1:T(8,128)(2,1)}, bf16[1,16,24,2048]{3,2,0,1:T(8,128)(2,1)S(1)}) fusion(bf16[4,16,24,2048]{3,2,0,1:T(8,128)(2,1)} %all-to-all-done), kind=kLoop, calls=%fused_computation.80 | loop fusion | bytes 12582912 | tf_op jit(solution)/shard_map/slice | solution.py:47
  134.3 3.5 fusion.23
  137.8 3.4 multiply_reduce_fusion.2
  141.4 4.1 %multiply_reduce_fusion.1 = f32[384]{0:T(512)S(1)} fusion(bf16[384,2048]{1,0:T(8,128)(2,1)} %bitcast.89, bf16[384,768]{1,0:T(8,128)(2,1)} %bitcast.102, bf16[4,2048,768]{2,1,0:T(8,128)(2,1)} %param.12), kind=kOutput, calls=%fused_computation.29 | convolution fusion | flops 1210318464 | bytes 5309952 | tf_op jit(solution)/shard_map/dot_general | solution.py:50
  145.6 3.9 multiply_reduce_fusion.3
  149.6 3.9 multiply_reduce_fusion
  154.2 5.4 %all-to-all-start.1 = ((f32[4,16,24]{2,0,1:T(4,128)}), f32[4,16,24]{2,0,1:T(4,128)S(1)}, u32[]{:S(2)}, u32[]{:S(2)}) async-start(f32[4,16,24]{2,0,1:T(4,128)} %pad_maximum_fusion.2), calls=%async_computation.2 | async-start | bytes 65536 | tf_op jit(solution)/shard_map/all_to_all | solution.py:67
  159.7 5.0 %fusion.24 = bf16[1,2048,768]{2,1,0:T(8,128)(2,1)} fusion(bf16[384,2048]{1,0:T(8,128)(2,1)} %bitcast.90, bf16[384,768]{1,0:T(8,128)(2,1)} %bitcast.103), kind=kOutput, calls=%fused_computation.35 | convolution fusion | flops 1209532416 | bytes 5308416 | tf_op jit(solution)/shard_map/dot_general | solution.py:58
  164.7 1.4 all-to-all-done.1
  166.2 6.2 %gather_fusion = f32[1024]{0:T(1024)S(1)} fusion(f32[1536]{0:T(1024)S(1)} %reshape.84, s32[1024]{0:T(1024)S(1)} %broadcast_clamp_fusion), kind=kCustom, calls=%fused_computation | custom fusion | bytes 12288 | tf_op jit(solution)/shard_map/gather | solution.py:69
  172.7 1.0 fusion.71
  174.0 5.0 %fusion.22 = bf16[1,2048,768]{2,1,0:T(8,128)(2,1)} fusion(bf16[384,2048]{1,0:T(8,128)(2,1)} %bitcast.93, bf16[384,768]{1,0:T(8,128)(2,1)S(1)} %bitcast.101), kind=kOutput, calls=%fused_computation.33 | convolution fusion | flops 1209532416 | bytes 5308416 | tf_op jit(solution)/shard_map/dot_general | solution.py:58
  179.0 3.5 fusion.25
  182.6 77.6 %all-reduce.3.cloned.1.call-done = f32[64,2048]{1,0:T(8,128)} async-done(((f32[64,2048]{1,0:T(8,128)}), f32[64,2048]{1,0:T(8,128)}) %all-reduce.3.cloned.1.call-update) | async-done | bytes 524304 | tf_op jit(solution)/shard_map/psum | solution.py:80
  260.2 10.7 %pad_maximum_fusion = bf16[4,2048,768]{2,1,0:T(8,128)(2,1)} fusion(bf16[1,2048,768]{2,1,0:T(8,128)(2,1)} %fusion.25, bf16[1,2048,768]{2,1,0:T(8,128)(2,1)} %fusion.24, bf16[1,2048,768]{2,1,0:T(8,128)(2,1)} %fusion.23, bf16[1,2048,768]{2,1,0:T(8,128)(2,1)} %fusion.22), kind=kLoop, calls=%fused_computation.2 | loop fusion | flops 18874368 | bytes 25165824 | tf_op jit(solution)/shard_map/stack | solution.py:63
  271.0 3.9 fusion.51
  274.9 3.4 fusion.42
  278.3 3.3 fusion.48
  281.7 3.3 fusion.45
  285.0 1.7 pad_maximum_fusion.1
  286.7 1.1 convolution_convert_fusion.4
  287.8 34.5 %all-reduce.5.cloned.1.call-done = f32[64,2048]{1,0:T(8,128)} async-done(((f32[64,2048]{1,0:T(8,128)}), f32[64,2048]{1,0:T(8,128)}) %all-reduce.5.cloned.1.call-update) | async-done | bytes 524304 | tf_op jit(solution)/shard_map/psum | solution.py:80
  322.3 76.0 %reduce-scatter.2.cloned.1.call-done = bf16[4,256,768]{2,1,0:T(8,128)(2,1)} async-done(((bf16[4,2048,768]{2,1,0:T(8,128)(2,1)}), bf16[4,256,768]{2,1,0:T(8,128)(2,1)}) %reduce-scatter.2.cloned.1.call-update) | async-done | bytes 1572880 | tf_op jit(solution)/shard_map/reduce_scatter | solution.py:62
  398.3 1.9 copy.53
  (48 shorter events, 4.0 us)
Async XLA Ops:
  7.2 165.5 %copy-start = (bf16[128,2048]{1,0:T(8,128)(2,1)S(1)}, bf16[128,2048]{1,0:T(8,128)(2,1)}, u32[]{:S(2)}) copy-start(bf16[128,2048]{1,0:T(8,128)(2,1)} %param.7) | copy-start | bytes 1572868
  29.0 8.0 %copy-start.1 = (bf16[1,4,16,24,768]{4,3,2,1,0:T(8,128)(2,1)S(1)}, bf16[1,4,16,24,768]{4,3,2,1,0:T(8,128)(2,1)}, u32[]{:S(2)}) copy-start(bf16[1,4,16,24,768]{4,3,2,1,0:T(8,128)(2,1)} %param.11) | copy-start | bytes 7077892
  29.0 100.1 %all-to-all-start = ((bf16[4,16,24,2048]{3,2,0,1:T(8,128)(2,1)}), bf16[4,16,24,2048]{3,2,0,1:T(8,128)(2,1)}, u32[]{:S(2)}, u32[]{:S(2)}) async-start(bf16[4,16,24,2048]{3,2,0,1:T(8,128)(2,1)} %copy.47), calls=%async_computation | async-start | bytes 12582912 | tf_op jit(solution)/shard_map/all_to_all | solution.py:41
  38.2 96.1 %copy-start.6 = (bf16[1,1,16,24,768]{4,3,2,1,0:T(8,128)(2,1)S(1)}, bf16[1,1,16,24,768]{4,3,2,1,0:T(8,128)(2,1)}, u32[]{:S(2)}) copy-start(bf16[1,1,16,24,768]{4,3,2,1,0:T(8,128)(2,1)} %get-tuple-element.11) | copy-start | bytes 1769476
  141.4 4.2 %copy-start.5 = (bf16[1,1,16,24,768]{4,3,2,1,0:T(8,128)(2,1)S(1)}, bf16[1,1,16,24,768]{4,3,2,1,0:T(8,128)(2,1)}, u32[]{:S(2)}) copy-start(bf16[1,1,16,24,768]{4,3,2,1,0:T(8,128)(2,1)} %get-tuple-element.10) | copy-start | bytes 1769476
  154.2 11.8 %all-to-all-start.1 = ((f32[4,16,24]{2,0,1:T(4,128)}), f32[4,16,24]{2,0,1:T(4,128)S(1)}, u32[]{:S(2)}, u32[]{:S(2)}) async-start(f32[4,16,24]{2,0,1:T(4,128)} %pad_maximum_fusion.2), calls=%async_computation.2 | async-start | bytes 65536 | tf_op jit(solution)/shard_map/all_to_all | solution.py:67
  159.6 100.6 %all-reduce.3.cloned.1.call-start = ((), (), s32[]{:S(2)}) async-start(), calls=%async_computation.4 | async-start | bytes 1048576 | tf_op jit(solution)/shard_map/psum | solution.py:80
  166.2 6.5 %copy-start.9 = (f32[128,8]{0,1:T(8,128)S(1)}, f32[128,8]{0,1:T(8,128)}, u32[]{:S(2)}) copy-start(f32[128,8]{0,1:T(8,128)} %param.9) | copy-start | bytes 12292
  166.2 6.5 %copy-start.8 = (s32[128,8]{0,1:T(8,128)S(1)}, s32[128,8]{0,1:T(8,128)}, u32[]{:S(2)}) copy-start(s32[128,8]{0,1:T(8,128)} %param.10) | copy-start | bytes 12292
  173.7 148.5 %all-reduce.5.cloned.1.call-start = ((), (), s32[]{:S(2)}) async-start(), calls=%async_computation.5 | async-start | bytes 1048576 | tf_op jit(solution)/shard_map/psum | solution.py:80
  174.0 5.0 %copy-start.4 = (bf16[1,16,24,2048]{3,2,0,1:T(8,128)(2,1)S(1)}, bf16[1,16,24,2048]{3,2,0,1:T(8,128)(2,1)}, u32[]{:S(2)}) copy-start(bf16[1,16,24,2048]{3,2,0,1:T(8,128)(2,1)} %get-tuple-element.7) | copy-start | bytes 4718596
  260.2 138.1 %reduce-scatter.2.cloned.1.call-start = ((), (), s32[]{:S(2)}) async-start(), calls=%async_computation.3 | async-start | bytes 14155776 | tf_op jit(solution)/shard_map/reduce_scatter | solution.py:62
  271.0 3.9 copy-start.3
  274.9 3.4 copy-start.2
  285.0 1.7 copy-start.7
Sparse Core Ops, SparseCore 0:
  173.8 86.2 all-reduce.2
  262.6 59.6 all-reduce.4
  325.3 72.9 reduce-scatter.1
